TPU v7x, 512 devices: a whole 4x4x16 slice. The times are simulated.
512 devices in a mesh: row: 8 (over z_lo), col: 16 (over x, y), layer: 4 (over z_hi, core).
Axes of the slice: x: 4, y: 4, z: 16 (z_hi: 2, z_lo: 8; z = z_hi * 8 + z_lo), core: 2. Of those that a mesh axis runs over, the one named last changes fastest.
Arguments:
- doubles_amplitude_tensor: float32 [2304, 2048], P('col', 'layer'), may hold values from -6 to 6
- integrals: float32 [8, 16, 4, 96, 2048], P('row', 'col', 'layer'), may hold values from -0.125 to 0.125
- incoming_residual: float32 [2304, 49152], P('col', ('row', 'layer')), may hold values from -6 to 6
Outputs:
- updated_residual: float32 [2304, 49152], P('col', ('row', 'layer'))
All inputs are finite; a program needn't handle non-finite values.
Results may differ from a plain program's by a relative error of at most 0.00005.
Values sent between devices are 32-bit elements; how exact they have to be, the bound alone decides.
No kernel may reach another device: no remote copies, remote signals or barrier semaphores. Data moves between devices by JAX's collectives and lax.ppermute only.
A program may use at most 64 MiB of HBM per device.

v0:
```python
import jax
import jax.numpy as jnp
from jax import lax
from jax.sharding import PartitionSpec as P


def regroup(integrals):
    local = integrals.reshape(1, integrals.shape[3], integrals.shape[4])
    return lax.all_to_all(local, "layer", split_axis=2, concat_axis=0, tiled=True)


def on_device(doubles_amplitude_tensor, integrals, incoming_residual):
    ij_rows = doubles_amplitude_tensor.shape[0]
    regrouped = regroup(integrals)[None]
    partial_ladder_value = jnp.einsum(
        "ic,nlkc->inlk",
        doubles_amplitude_tensor,
        lax.all_gather(regrouped, "col", axis=0, tiled=True),
        precision=lax.Precision.HIGHEST,
        preferred_element_type=jnp.float32,
    )
    summed = lax.psum_scatter(partial_ladder_value, "layer", scatter_dimension=2, tiled=True)
    return incoming_residual + summed.reshape(ij_rows, -1)


def solution(mesh):
    return jax.shard_map(
        on_device,
        mesh=mesh,
        in_specs=(
            P("col", "layer"),
            P("row", "col", "layer", None, None),
            P("col", ("row", "layer")),
        ),
        out_specs=P("col", ("row", "layer")),
        check_vma=False,
    )
```

profile of v0, /device:TPU:1, one launch (start us, length us, event | category | flops | bytes accessed | tf_op | source)
XLA Modules:
  0.0 565.8 jit_solution(12398285052435293716)
XLA Ops:
  6.5 0.0 copy-start
  6.5 0.0 all-gather.3.cloned.1.call-start
  6.5 1.5 copy.7
  8.1 43.3 %all_to_all.15 = f32[1,96,2048]{1,0,2:T(1,128)S(1)} all-to-all(f32[1,96,2048]{1,0,2:T(1,128)S(1)} %bitcast.24), channel_id=1, replica_groups=mesh['row'=8,'col'=16,'layer'=4] {'layer'}, dimensions={2} | all-to-all | bytes 1572864 | tf_op jit(solution)/shard_map/all_to_all | solution.py:9
  51.4 1.2 copy.8
  52.6 0.0 all-gather.3.cloned.1.call-update
  52.6 0.0 all-reduce.3.cloned.1.call-start
  52.6 128.7 %all-gather.3.cloned.1.call-done = f32[64,1,96,512]{3,2,1,0:T(8,128)} async-done(((f32[4,1,96,512]{3,2,1,0:T(8,128)}), f32[64,1,96,512]{3,2,1,0:T(8,128)}) %all-gather.3.cloned.1.call-update) | async-done | bytes 12582928 | tf_op jit(solution)/shard_map/all_gather | solution.py:18
  181.3 0.0 copy-done
  181.4 18.7 %fusion = f32[144,16,4,96]{3,0,2,1:T(8,128)} fusion(f32[144,512]{1,0:T(8,128)S(1)} %copy-done, f32[16,4,96,512]{3,2,1,0:T(8,128)} %bitcast.22), kind=kOutput, calls=%fused_computation | convolution fusion | flops 5435817984 | bytes 16416768 | tf_op jit(solution)/shard_map/ic,nlkc->inlk/dot_general | solution.py:15
  200.1 0.0 copy-start.1
  200.1 0.0 all-reduce.3.cloned.1.call-update
  200.1 1.3 dynamic-slice
  201.5 353.6 %all-reduce.3.cloned.1.call-done = f32[144,16,4,96]{3,0,2,1:T(8,128)} async-done(((f32[144,16,4,96]{3,0,2,1:T(8,128)}), f32[144,16,4,96]{3,0,2,1:T(8,128)}) %all-reduce.3.cloned.1.call-update) | async-done | bytes 3538960
  555.1 2.0 constant_dynamic-slice_fusion
  557.1 0.4 copy.9
  557.5 0.5 reshape.8
  558.0 0.0 copy-done.1
  558.0 1.0 add.5
Async XLA Ops:
  6.5 174.8 %copy-start = (f32[144,512]{1,0:T(8,128)S(1)}, f32[144,512]{1,0:T(8,128)}, u32[]{:S(2)}) copy-start(f32[144,512]{1,0:T(8,128)} %param.3) | copy-start | bytes 884740
  6.5 174.8 %all-gather.3.cloned.1.call-start = ((), (), s32[]{:S(2)}) async-start(), calls=%async_computation.1 | async-start | bytes 13369344 | tf_op jit(solution)/shard_map/all_gather | solution.py:18
  52.6 502.5 %all-reduce.3.cloned.1.call-start = ((), (), s32[]{:S(2)}) async-start(), calls=%async_computation.2 | async-start | bytes 9437184
  200.1 357.9 %copy-start.1 = (f32[144,1536]{1,0:T(8,128)S(1)}, f32[144,1536]{1,0:T(8,128)}, u32[]{:S(2)}) copy-start(f32[144,1536]{1,0:T(8,128)} %param.5) | copy-start | bytes 2654212
Sparse Core Ops, SparseCore 0:
  52.7 128.5 all-gather.2
  200.2 354.7 all-reduce.2
where the time goes:
time: 566 us
  waiting for transfers between devices  482 us (85%)
  blocking collectives  43.3 us (8%)
  matrix products  18.7 us (3%)
  between operations  13.4 us (2%)
  local copies, waits for them, and re-layouts  6.95 us (1%)
    unnamed x3, waiting for transfers between devices  354 us
    all_gather x1, waiting for transfers between devices, on_device(): lax.all_gather(regrouped, 'col', axis=0, tiled=True)  129 us
    all_to_all x1, blocking collectives, regroup(): lax.all_to_all(local, 'layer', split_axis=2, concat_axis=0, tiled=True)  43.3 us
    dot_general x1, matrix products, on_device(): jnp.einsum('ic,nlkc->inlk', doubles_amplitude_tensor, lax.all_gather(regr...  18.7 us
  transfers between devices with their start and end apart: 2, of which 2 were waited for; matrix products, arithmetic and copies ran while one was open for 0% of the time, Pallas kernels for 0%

commit v1 on v0

--- a/solution.py
+++ b/solution.py
@@ -2,6 +2,16 @@
 import jax.numpy as jnp
 from jax import lax
 from jax.sharding import PartitionSpec as P
+
+
+def derive_series_all_for(x_in):
+    pieces_in = []
+    for _ in range(lax.axis_size("col")):
+        pieces_in.append(x_in)
+    finding = jnp.concatenate(
+        lax.all_to_all(jnp.stack(pieces_in), axis_name="col", concat_axis=0, split_axis=0), 0
+    )
+    return finding
 
 
 def regroup(integrals):
@@ -15,7 +25,7 @@
     partial_ladder_value = jnp.einsum(
         "ic,nlkc->inlk",
         doubles_amplitude_tensor,
-        lax.all_gather(regrouped, "col", axis=0, tiled=True),
+        derive_series_all_for(regrouped),
         precision=lax.Precision.HIGHEST,
         preferred_element_type=jnp.float32,
     )

time: 566 us -> 605 us (1.069)
  blocking collectives: 43.3 us -> 188 us
  waiting for transfers between devices: 482 us -> 377 us
    all_to_all x0 -> x1, blocking collectives: none -> 145 us  [derive_series_all_for(): lax.all_to_all(jnp.stack(pieces_in), axis_name='col', concat_axis=0, spli...]
    all_gather x1 -> x0, waiting for transfers between devices: 129 us -> none  [on_device(): lax.all_gather(regrouped, 'col', axis=0, tiled=True)]
    unnamed x3 -> x2, waiting for transfers between devices: 354 us -> 377 us
  transfers between devices with their start and end apart: 2 -> 1, of which waited for: 2 -> 1; matrix products, arithmetic and copies ran while one was open for 0% -> 0% of each run, Pallas kernels for 0% -> 0%
where the time goes in v1:
time: 605 us; the launch traced here: 604 us
  waiting for transfers between devices  377 us (62%)
  blocking collectives  188 us (31%)
  matrix products  17.2 us (3%)
  between operations  13.4 us (2%)
  local copies, waits for them, and re-layouts  7.66 us (1%)
    unnamed x2, waiting for transfers between devices  377 us
    all_to_all x1, blocking collectives, derive_series_all_for(): lax.all_to_all(jnp.stack(pieces_in), axis_name='col', concat_axis=0, spli...  145 us
    all_to_all x1, blocking collectives, regroup(): lax.all_to_all(local, 'layer', split_axis=2, concat_axis=0, tiled=True)  43.3 us
    dot_general x1, matrix products, on_device(): jnp.einsum('ic,nlkc->inlk', doubles_amplitude_tensor, derive_series_all_f...  17.2 us
  transfers between devices with their start and end apart: 1, of which 1 were waited for; matrix products, arithmetic and copies ran while one was open for 0% of the time, Pallas kernels for 0%

profile of v1, /device:TPU:1, one launch (start us, length us, event | category | flops | bytes accessed | tf_op | source)
XLA Modules:
  0.0 604.4 jit_solution(758456448649994578)
XLA Ops:
  6.5 0.0 copy-start
  6.5 0.0 all-reduce.3.cloned.1.call-start
  6.5 1.5 copy.7
  8.1 43.3 %all_to_all.20 = f32[1,96,2048]{1,0,2:T(1,128)S(1)} all-to-all(f32[1,96,2048]{1,0,2:T(1,128)S(1)} %bitcast.24), channel_id=1, replica_groups=mesh['row'=8,'col'=16,'layer'=4] {'layer'}, dimensions={2} | all-to-all | bytes 1572864 | tf_op jit(solution)/shard_map/all_to_all | solution.py:19
  51.4 0.3 copy.8
  51.7 1.6 stack.3
  53.3 144.8 %all_to_all.21 = f32[16,1,4,96,512]{4,3,2,1,0:T(8,128)S(1)} all-to-all(f32[16,1,4,96,512]{4,3,2,1,0:T(8,128)S(1)} %stack.3), channel_id=1, replica_groups=mesh['row'=8,'col'=16,'layer'=4] {'col'}, dimensions={0} | all-to-all | bytes 25165824 | tf_op jit(solution)/shard_map/all_to_all | solution.py:12
  198.1 0.0 copy-done
  198.1 17.2 %fusion = f32[144,16,4,96]{3,0,2,1:T(8,128)} fusion(f32[16,1,4,96,512]{4,3,2,1,0:T(8,128)S(1)} %all_to_all.21, f32[144,512]{1,0:T(8,128)S(1)} %copy-done), kind=kOutput, calls=%fused_computation | convolution fusion | flops 5435817984 | bytes 16416768 | tf_op jit(solution)/shard_map/ic,nlkc->inlk/dot_general | solution.py:25
  215.3 0.0 copy-start.1
  215.3 0.0 all-reduce.3.cloned.1.call-update
  215.3 1.3 dynamic-slice
  216.7 376.9 %all-reduce.3.cloned.1.call-done = f32[144,16,4,96]{3,0,2,1:T(8,128)} async-done(((f32[144,16,4,96]{3,0,2,1:T(8,128)}), f32[144,16,4,96]{3,0,2,1:T(8,128)}) %all-reduce.3.cloned.1.call-update) | async-done | bytes 3538960
  593.6 2.0 constant_dynamic-slice_fusion
  595.6 0.4 copy.9
  596.0 0.5 reshape.16
  596.5 0.0 copy-done.1
  596.5 1.0 add.5
Async XLA Ops:
  6.5 191.5 %copy-start = (f32[144,512]{1,0:T(8,128)S(1)}, f32[144,512]{1,0:T(8,128)}, u32[]{:S(2)}) copy-start(f32[144,512]{1,0:T(8,128)} %param.3) | copy-start | bytes 884740
  6.5 587.1 %all-reduce.3.cloned.1.call-start = ((), (), s32[]{:S(2)}) async-start(), calls=%async_computation.2 | async-start | bytes 9437184
  215.3 381.2 %copy-start.1 = (f32[144,1536]{1,0:T(8,128)S(1)}, f32[144,1536]{1,0:T(8,128)}, u32[]{:S(2)}) copy-start(f32[144,1536]{1,0:T(8,128)} %param.5) | copy-start | bytes 2654212
Sparse Core Ops, SparseCore 0:
  215.4 378.1 all-reduce.2
